TPU v7x, 512 devices: a whole 4x4x16 slice. The times are simulated.
512 devices in a mesh: batch: 32 (over z, core), row: 4 (over y), col: 4 (over x).
Axes of the slice: x: 4, y: 4, z: 16, core: 2. Of those that a mesh axis runs over, the one named last changes fastest.
Arguments:
- image_tokens: bfloat16 [128, 256, 3072], P('batch', ('row', 'col')), may hold values from -36 to 36
- text_tokens: bfloat16 [128, 128, 3072], P('batch', ('row', 'col')), may hold values from -36 to 36
- modulation: float32 [128, 7, 3072], P('batch'), may hold values from -3.5 to 3.5
- qkv_weight: bfloat16 [3072, 12, 384], P('col', 'row'), may hold values from -0.109375 to 0.109375
- kv_weight: bfloat16 [3072, 12, 256], P('col', 'row'), may hold values from -0.109375 to 0.109375
- norm_gains: float32 [3, 128], replicated, may hold values from 1 to 2.2
- out_weight: bfloat16 [12, 128, 3072], P('row', None, 'col'), may hold values from -0.15625 to 0.15625
- final_weight: bfloat16 [3072, 64], replicated, may hold values from -0.109375 to 0.109375
- text_lengths: int32 [128], P('batch'), may hold values from 1 to 128, as said below
- partner: int32 [128], P('batch'), may hold values from 0 to 127, as said below
- guidance: float32 [128], P('batch'), may hold values from 1.5 to 4.5
- step_size: float32 [128], P('batch'), may hold values from -0.3 to -0.05
- latent: float32 [128, 256, 64], P('batch', ('row', 'col')), may hold values from -6 to 6
Outputs:
- next_latent: float32 [128, 256, 64], P('batch', ('row', 'col'))
Inputs may be any that keep to these rules, and one draw needn't show every extreme that they name: `text_lengths`: some sequence has all 128 text tokens live. partner[partner[s]] = s and partner[s] != s for every sequence s.
All inputs are finite; a program needn't handle non-finite values.
Results may differ from a plain program's by a relative error of at most 0.007.
Values may be sent and summed in bfloat16 or wider, within the bound.
No kernel may reach another device: no remote copies, remote signals or barrier semaphores. Data moves between devices by JAX's collectives and lax.ppermute only.
A program may use at most 64 MiB of HBM per device.

v0:
```python
import math
import jax
import jax.numpy as jnp
from jax import lax
from jax.sharding import PartitionSpec as P

epsilon = 1e-06


def layer_norm(values):
    center = jnp.mean(values, axis=-1, keepdims=True)
    spread = jnp.mean((values - center) * (values - center), axis=-1, keepdims=True)
    return (values - center) * lax.rsqrt(spread + epsilon)


def modulate(values, shift, scale):
    return layer_norm(values) * (1.0 + scale[:, None, :]) + shift[:, None, :]


def head_norm(values, gain):
    return values * lax.rsqrt(jnp.mean(values * values, axis=-1, keepdims=True) + epsilon) * gain


def attend(queries, all_keys, all_values, live, head_size):
    scores = jnp.einsum(
        "sqhe,skhe->shqk", queries, all_keys, preferred_element_type=jnp.float32
    ) / math.sqrt(head_size)
    expo = jnp.exp(scores) * live[:, None, None, :]
    totals = jnp.sum(expo, axis=-1)
    mixed = jnp.einsum(
        "shqk,skhe->sqhe", expo.astype(jnp.bfloat16), all_values, preferred_element_type=jnp.float32
    )
    return (mixed / jnp.transpose(totals, (0, 2, 1))[..., None]).astype(jnp.bfloat16)


def per_device(
    image_tokens,
    text_tokens,
    modulation,
    qkv_weight,
    kv_weight,
    norm_gains,
    out_weight,
    final_weight,
    text_lengths,
    partner,
    guidance,
    step_size,
    latent,
):
    count = image_tokens.shape[0]
    head_size = norm_gains.shape[1]
    block_width = qkv_weight.shape[0]
    image_mod = modulate(
        image_tokens.astype(jnp.float32), modulation[:, 0], modulation[:, 1]
    ).astype(jnp.bfloat16)
    text_mod = modulate(text_tokens.astype(jnp.float32), modulation[:, 3], modulation[:, 4]).astype(
        jnp.bfloat16
    )
    image_whole, text_whole = (
        lax.all_gather(image_mod, ("row", "col"), axis=1, tiled=True),
        lax.all_gather(text_mod, ("row", "col"), axis=1, tiled=True),
    )
    offset = lax.axis_index("col") * block_width
    image_all = lax.dynamic_slice_in_dim(image_whole, offset, block_width, 2)
    text_all = lax.dynamic_slice_in_dim(text_whole, offset, block_width, 2)
    qkv_term = jnp.einsum(
        "std,dhe->sthe", image_all, qkv_weight, preferred_element_type=jnp.float32
    )
    kv_term = jnp.einsum("std,dhe->sthe", text_all, kv_weight, preferred_element_type=jnp.float32)
    qkv_sum, kv_sum = (
        lax.psum(qkv_term.astype(jnp.bfloat16), "col").astype(jnp.float32),
        lax.psum(kv_term.astype(jnp.bfloat16), "col").astype(jnp.float32),
    )
    queries = head_norm(qkv_sum[..., :head_size], norm_gains[0]).astype(jnp.bfloat16)
    image_keys = head_norm(qkv_sum[..., head_size : 2 * head_size], norm_gains[1]).astype(
        jnp.bfloat16
    )
    image_values = qkv_sum[..., 2 * head_size :].astype(jnp.bfloat16)
    text_keys = head_norm(kv_sum[..., :head_size], norm_gains[2]).astype(jnp.bfloat16)
    text_values = kv_sum[..., head_size:].astype(jnp.bfloat16)
    text_count = text_keys.shape[1]
    image_count = image_keys.shape[1]
    all_keys = jnp.concatenate([text_keys, image_keys], axis=1)
    all_values = jnp.concatenate([text_values, image_values], axis=1)
    text_live = (jnp.arange(text_count, dtype=jnp.int32)[None, :] < text_lengths[:, None]).astype(
        jnp.float32
    )
    live = jnp.concatenate([text_live, jnp.ones((count, image_count), jnp.float32)], axis=1)
    heads = attend(queries, all_keys, all_values, live, head_size)
    out_term = jnp.einsum("sqhe,hed->sqd", heads, out_weight, preferred_element_type=jnp.float32)
    attn_rows = lax.psum_scatter(
        out_term.astype(jnp.bfloat16), "row", scatter_dimension=1, tiled=True
    )
    attn_tokens = lax.all_to_all(attn_rows, "col", split_axis=1, concat_axis=2, tiled=True)
    residual = image_tokens.astype(jnp.float32) + modulation[:, 2][:, None, :] * attn_tokens.astype(
        jnp.float32
    )
    final_in = modulate(residual, modulation[:, 5], modulation[:, 6]).astype(jnp.bfloat16)
    velocity = jnp.einsum("std,dc->stc", final_in, final_weight, preferred_element_type=jnp.float32)
    token_rows = velocity.shape[1]
    channels = velocity.shape[2]
    flat_velocity = velocity.reshape(count, token_rows * channels)
    every_velocity, every_guidance = (
        lax.all_gather(flat_velocity, "batch", axis=0, tiled=True),
        lax.all_gather(guidance, "batch", axis=0, tiled=True),
    )
    mate = jnp.take(every_velocity, partner, axis=0).reshape(velocity.shape)
    own_index = lax.axis_index("batch") * count + jnp.arange(count, dtype=jnp.int32)
    is_cond = own_index < partner
    cond_vel = jnp.where(is_cond[:, None, None], velocity, mate)
    uncond_vel = jnp.where(is_cond[:, None, None], mate, velocity)
    scale_guide = jnp.where(is_cond, guidance, jnp.take(every_guidance, partner))
    guided = uncond_vel + scale_guide[:, None, None] * (cond_vel - uncond_vel)
    ratio = jnp.sqrt(
        (jnp.mean(cond_vel * cond_vel, axis=-1, keepdims=True) + epsilon)
        / (jnp.mean(guided * guided, axis=-1, keepdims=True) + epsilon)
    )
    return latent + step_size[:, None, None] * guided * (0.7 * ratio + 0.3)


def solution(mesh):
    return jax.shard_map(
        per_device,
        mesh=mesh,
        in_specs=(
            P("batch", ("row", "col"), None),
            P("batch", ("row", "col"), None),
            P("batch", None, None),
            P("col", "row", None),
            P("col", "row", None),
            P(),
            P("row", None, "col"),
            P(),
            P("batch"),
            P("batch"),
            P("batch"),
            P("batch"),
            P("batch", ("row", "col"), None),
        ),
        out_specs=P("batch", ("row", "col"), None),
        check_vma=False,
    )
```

profile of v0, /device:TPU:1, one launch (start us, length us, event | category | flops | bytes accessed | tf_op | source)
XLA Modules:
  0.0 376.6 jit_solution(10970847019949007939)
XLA Ops:
  6.5 1.2 convert_reduce_fusion.1
  7.7 1.1 fusion.42
  8.9 1.0 slice_bitcast_fusion.3
  9.9 1.8 fusion.45
  11.6 0.0 all-gather.4.cloned.1.call-update
  11.7 0.0 all-gather.6.cloned.1.call-start
  11.7 1.1 convert_reduce_fusion
  12.8 0.2 fusion.27
  13.1 1.0 fusion.30
  14.1 0.0 all-reduce.5.cloned.1.call-start
  14.2 65.4 %all-gather.4.cloned.1.call-done = bf16[4,128,3072]{2,1,0:T(8,128)(2,1)} async-done(((bf16[4,8,3072]{2,1,0:T(8,128)(2,1)}), bf16[4,128,3072]{2,1,0:T(8,128)(2,1)}) %all-gather.4.cloned.1.call-update) | async-done | bytes 3145744 | tf_op jit(solution)/shard_map/all_gather | solution.py:62
  79.6 3.2 convolution_convert_fusion.1
  82.7 75.8 %all-gather.6.cloned.1.call-done = bf16[4,256,3072]{2,1,0:T(8,128)(2,1)} async-done(((bf16[4,16,3072]{2,1,0:T(8,128)(2,1)}), bf16[4,256,3072]{2,1,0:T(8,128)(2,1)}) %all-gather.6.cloned.1.call-update) | async-done | bytes 6291472 | tf_op jit(solution)/shard_map/all_gather | solution.py:61
  158.5 5.0 %convolution_convert_fusion = bf16[4,256,3,384]{3,1,2,0:T(8,128)(2,1)} fusion(bf16[768,3,384]{2,0,1:T(8,128)(2,1)S(1)} %copy-done, bf16[4,256,3072]{2,1,0:T(8,128)(2,1)} %all-gather.6.cloned.1.call-done, s32[]{:T(128)S(6)} %select_n.32), kind=kOutput, calls=%fused_computation.9 | convolution fusion | flops 1813118976 | bytes 5701636 | tf_op jit(solution)/shard_map/std,dhe->sthe/dot_general | solution.py:67
  163.6 0.0 reduce-scatter.2.cloned.1.call-start
  163.6 0.6 copy-done.9
  164.2 0.1 iota_compare_fusion
  164.3 90.3 %all-reduce.5.cloned.1.call-done = (bf16[4,256,3,384]{3,1,2,0:T(8,128)(2,1)}, bf16[4,128,3,256]{3,1,2,0:T(8,128)(2,1)}) async-done(((bf16[4,256,3,384]{3,1,2,0:T(8,128)(2,1)}, bf16[4,128,3,256]{3,1,2,0:T(8,128)(2,1)}), (bf16[4,256,3,384]{3,1,2,0:T(8,128)(2,1)}, bf16[4,128,3,256]{3,1,2,0:T(8,128)(2,1)})) %all-reduce.5.cloned.1.call-update) | async-done | bytes 3145744 | tf_op jit(solution)/shard_map/psum | solution.py:72
  254.6 1.4 fusion.31
  256.0 1.0 slice.70
  257.1 1.2 slice.71
  258.3 0.4 convert_element_type.65
  258.7 0.9 multiply_reduce_fusion.1
  259.6 0.2 copy-done.3
  259.9 0.3 fusion.33
  260.2 0.5 multiply_convert_fusion
  260.6 2.8 fusion
  263.4 5.8 %bitcast_convert_fusion = bf16[4,256,768]{2,1,0:T(8,128)(2,1)} fusion(f32[4,3,256,384]{3,2,1,0:T(8,128)} %get-tuple-element.25, f32[4,384]{1,0:T(4,128)S(1)} %pad_convert_fusion, bf16[4,256,3,128]{3,1,2,0:T(8,128)(2,1)S(1)} %slice.71, bf16[4,128,3,128]{3,1,2,0:T(8,128)(2,1)S(1)} %slice.70, f32[4,256,3]{1,2,0:T(4,128)S(1)} %bitcast.60, ...), kind=kOutput, calls=%fused_computation.5 | convolution fusion | flops 913440768 | bytes 8079360 | tf_op jit(solution)/shard_map/sqhe,hed->sqd/dot_general | solution.py:91
  269.2 1.3 dynamic-slice
  271.2 0.2 dynamic-update-slice
  271.4 48.1 %all-reduce.1 = f32[128]{0:T(128)S(1)} all-reduce(f32[128]{0:T(128)S(1)} %dynamic-update-slice), channel_id=1, replica_groups=mesh['batch'=32,'row'=4,'col'=4] {'batch'}, use_global_device_ids=true, to_apply=%add.1 | all-reduce | flops 128 | bytes 1024
  319.6 0.0 reduce-scatter.2.cloned.1.call-done
  319.6 2.0 copy.18
  321.6 3.5 all-to-all-start
  325.1 0.6 gather_fusion.1
  325.8 5.5 %all-to-all-done = bf16[4,64,768]{2,0,1:T(4,128)(2,1)S(1)} async-done(((bf16[4,64,768]{2,0,1:T(4,128)(2,1)}), bf16[4,64,768]{2,0,1:T(4,128)(2,1)S(1)}, u32[]{:S(2)}, u32[]{:S(2)}) %all-to-all-start) | async-done | bytes 393248 | tf_op jit(solution)/shard_map/all_to_all | solution.py:95
  331.3 1.2 copy.26
  332.5 1.5 reshape.109
  334.0 0.2 fusion.52
  334.2 0.3 multiply_reduce_fusion.2
  334.5 1.4 fusion.46
  335.9 0.1 reshape.132
  336.0 32.3 %all-gather = f32[32,4,1024]{2,1,0:T(4,128)S(1)} all-gather(f32[1,4,1024]{2,1,0:T(4,128)S(1)} %reshape.132), channel_id=1, replica_groups=mesh['batch'=32,'row'=4,'col'=4] {'batch'}, dimensions={0}, use_global_device_ids=true | all-gather | bytes 540672 | tf_op jit(solution)/shard_map/all_gather | solution.py:105
  368.3 0.2 reshape.133
  368.5 0.6 gather_fusion
  369.1 0.1 gather.11
  369.2 0.2 multiply_reduce_fusion.3
  369.4 0.7 multiply_add_fusion
  (38 shorter events, 0.2 us)
Async XLA Ops:
  6.5 152.0 %copy-start = (bf16[768,3,384]{2,0,1:T(8,128)(2,1)S(1)}, bf16[768,3,384]{2,0,1:T(8,128)(2,1)}, u32[]{:S(2)}) copy-start(bf16[768,3,384]{2,0,1:T(8,128)(2,1)} %param.16) | copy-start | bytes 5308420
  6.5 6.3 %copy-start.1 = (bf16[4,16,3072]{2,1,0:T(8,128)(2,1)S(1)}, bf16[4,16,3072]{2,1,0:T(8,128)(2,1)}, u32[]{:S(2)}) copy-start(bf16[4,16,3072]{2,1,0:T(8,128)(2,1)} %param.13) | copy-start | bytes 1179652
  6.5 73.0 %all-gather.4.cloned.1.call-start = ((), (), s32[]{:S(2)}) async-start(), calls=%async_computation.2 | async-start | bytes 3342336 | tf_op jit(solution)/shard_map/all_gather | solution.py:62
  11.7 146.9 %all-gather.6.cloned.1.call-start = ((), (), s32[]{:S(2)}) async-start(), calls=%async_computation.3 | async-start | bytes 6684672 | tf_op jit(solution)/shard_map/all_gather | solution.py:61
  14.1 240.5 %all-reduce.5.cloned.1.call-start = ((), (), s32[]{:S(2)}) async-start(), calls=%async_computation.5 | async-start | bytes 6291456 | tf_op jit(solution)/shard_map/psum | solution.py:72
  163.5 0.7 copy-start.9
  163.5 0.7 copy-start.5
  163.6 156.0 %reduce-scatter.2.cloned.1.call-start = ((), (), s32[]{:S(2)}) async-start(), calls=%async_computation.4 | async-start | bytes 1966080 | tf_op jit(solution)/shard_map/reduce_scatter | solution.py:92
  254.6 3.7 copy-start.2
  258.7 1.1 copy-start.3
  263.4 7.7 %copy-start.7 = (f32[4]{0:T(128)S(1)}, f32[4]{0:T(128)}, u32[]{:S(2)}) copy-start(f32[4]{0:T(128)} %param.23) | copy-start | bytes 52
  263.4 56.1 %copy-start.8 = (s32[4]{0:T(128)S(1)}, s32[4]{0:T(128)}, u32[]{:S(2)}) copy-start(s32[4]{0:T(128)} %param.22) | copy-start | bytes 52
  321.6 9.7 %all-to-all-start = ((bf16[4,64,768]{2,0,1:T(4,128)(2,1)}), bf16[4,64,768]{2,0,1:T(4,128)(2,1)S(1)}, u32[]{:S(2)}, u32[]{:S(2)}) async-start(bf16[4,64,768]{2,0,1:T(4,128)(2,1)} %copy.18), calls=%async_computation.1 | async-start | bytes 786432 | tf_op jit(solution)/shard_map/all_to_all | solution.py:95
  334.2 35.1 %copy-start.4 = (f32[4,16,64]{2,1,0:T(8,128)S(1)}, f32[4,16,64]{2,1,0:T(8,128)}, u32[]{:S(2)}) copy-start(f32[4,16,64]{2,1,0:T(8,128)} %param.25) | copy-start | bytes 49156
  334.2 35.1 %copy-start.6 = (f32[4]{0:T(128)S(1)}, f32[4]{0:T(128)}, u32[]{:S(2)}) copy-start(f32[4]{0:T(128)} %param.24) | copy-start | bytes 52
Sparse Core Ops, SparseCore 0:
  11.8 67.7 all-gather.3
  82.6 75.8 all-gather.5
  163.7 90.8 all-reduce.4
  269.3 32.5 reduce-scatter.1
where the time goes:
time: 377 us
  waiting for transfers between devices  237 us (63%)
  blocking collectives  80.4 us (21%)
  matrix products  18.2 us (5%)
  between operations  14 us (4%)
  other arithmetic  12.5 us (3%)
  local copies, waits for them, and re-layouts  10.9 us (3%)
    psum x1, waiting for transfers between devices, per_device(): lax.psum(qkv_term.astype(jnp.bfloat16), 'col').astype(jnp.float32)  90.3 us
    all_gather x1, waiting for transfers between devices, per_device(): lax.all_gather(image_mod, ('row', 'col'), axis=1, tiled=True)  75.8 us
    all_gather x1, waiting for transfers between devices, per_device(): lax.all_gather(text_mod, ('row', 'col'), axis=1, tiled=True)  65.4 us
    unnamed x1, blocking collectives  48.1 us
    all_gather x1, blocking collectives, per_device(): lax.all_gather(flat_velocity, 'batch', axis=0, tiled=True)  32.3 us
  transfers between devices with their start and end apart: 5, of which 4 were waited for; matrix products, arithmetic and copies ran while one was open for 2% of the time, Pallas kernels for 0%

commit v1 on v0

--- a/solution.py
+++ b/solution.py
@@ -48,6 +48,15 @@
     step_size,
     latent,
 ):
+
+    def remake_set_for(t0):
+        return jnp.concatenate(
+            jax.lax.all_to_all(
+                jnp.stack([t0 for _ in range(jax.lax.axis_size("batch"))], axis=0), "batch", 0, 0
+            ),
+            0,
+        )
+
     count = image_tokens.shape[0]
     head_size = norm_gains.shape[1]
     block_width = qkv_weight.shape[0]
@@ -102,7 +111,7 @@
     channels = velocity.shape[2]
     flat_velocity = velocity.reshape(count, token_rows * channels)
     every_velocity, every_guidance = (
-        lax.all_gather(flat_velocity, "batch", axis=0, tiled=True),
+        remake_set_for(flat_velocity),
         lax.all_gather(guidance, "batch", axis=0, tiled=True),
     )
     mate = jnp.take(every_velocity, partner, axis=0).reshape(velocity.shape)

time: 377 us -> 408 us (1.082)
  waiting for transfers between devices: 237 us -> 264 us
  starting transfers between devices: 3.59 us -> 15.5 us
  blocking collectives: 80.4 us -> 71.7 us
    reduce_scatter x1, waiting for transfers between devices: 0.02 us -> 32.7 us  [per_device(): lax.psum_scatter(out_term.astype(jnp.bfloat16), 'row', scatter_dimension=...]
    all_gather x1 -> x0, blocking collectives: 32.3 us -> none  [per_device(): lax.all_gather(flat_velocity, 'batch', axis=0, tiled=True)]
    unnamed x1, blocking collectives: 48.1 us -> 61.7 us
    all_to_all x1, starting transfers between devices: 3.46 us -> 15.3 us  [remake_set_for(): jax.lax.all_to_all(jnp.stack([t0 for _ in range(jax.lax.axis_size('batch'...]
    all_to_all x0 -> x1, blocking collectives: none -> 10 us  [per_device(): lax.all_to_all(attn_rows, 'col', split_axis=1, concat_axis=2, tiled=True)]
    all_to_all x1, waiting for transfers between devices: 5.53 us -> 0.01 us  [remake_set_for(): jax.lax.all_to_all(jnp.stack([t0 for _ in range(jax.lax.axis_size('batch'...]
where the time goes in v1:
time: 408 us; the launch traced here: 407 us
  waiting for transfers between devices  264 us (65%)
  blocking collectives  71.7 us (18%)
  matrix products  18.1 us (4%)
  starting transfers between devices  15.5 us (4%)
  between operations  14 us (3%)
  other arithmetic  12.4 us (3%)
  local copies, waits for them, and re-layouts  11 us (3%)
    psum x1, waiting for transfers between devices, per_device(): lax.psum(qkv_term.astype(jnp.bfloat16), 'col').astype(jnp.float32)  90.3 us
    all_gather x1, waiting for transfers between devices, per_device(): lax.all_gather(image_mod, ('row', 'col'), axis=1, tiled=True)  75.8 us
    all_gather x1, waiting for transfers between devices, per_device(): lax.all_gather(text_mod, ('row', 'col'), axis=1, tiled=True)  65.4 us
    unnamed x1, blocking collectives  61.7 us
    reduce_scatter x1, waiting for transfers between devices, per_device(): lax.psum_scatter(out_term.astype(jnp.bfloat16), 'row', scatter_dimension=...  32.7 us
    all_to_all x1, starting transfers between devices, remake_set_for(): jax.lax.all_to_all(jnp.stack([t0 for _ in range(jax.lax.axis_size('batch'...  15.3 us
    all_to_all x1, blocking collectives, per_device(): lax.all_to_all(attn_rows, 'col', split_axis=1, concat_axis=2, tiled=True)  10 us
  transfers between devices with their start and end apart: 5, of which 4 were waited for; matrix products, arithmetic and copies ran while one was open for 2% of the time, Pallas kernels for 0%

profile of v1, /device:TPU:1, one launch (start us, length us, event | category | flops | bytes accessed | tf_op | source)
XLA Modules:
  0.0 407.1 jit_solution(13255461365807404248)
XLA Ops:
  6.5 1.2 convert_reduce_fusion.1
  7.7 1.1 fusion.42
  8.9 1.0 slice_bitcast_fusion.3
  9.9 1.8 fusion.45
  11.6 0.0 all-gather.3.cloned.1.call-update
  11.7 0.0 all-gather.5.cloned.1.call-start
  11.7 1.1 convert_reduce_fusion
  12.8 0.2 fusion.27
  13.1 1.0 fusion.30
  14.1 0.0 all-reduce.5.cloned.1.call-start
  14.2 65.4 %all-gather.3.cloned.1.call-done = bf16[4,128,3072]{2,1,0:T(8,128)(2,1)} async-done(((bf16[4,8,3072]{2,1,0:T(8,128)(2,1)}), bf16[4,128,3072]{2,1,0:T(8,128)(2,1)}) %all-gather.3.cloned.1.call-update) | async-done | bytes 3145744 | tf_op jit(solution)/shard_map/all_gather | solution.py:71
  79.6 3.2 convolution_convert_fusion.1
  82.7 75.8 %all-gather.5.cloned.1.call-done = bf16[4,256,3072]{2,1,0:T(8,128)(2,1)} async-done(((bf16[4,16,3072]{2,1,0:T(8,128)(2,1)}), bf16[4,256,3072]{2,1,0:T(8,128)(2,1)}) %all-gather.5.cloned.1.call-update) | async-done | bytes 6291472 | tf_op jit(solution)/shard_map/all_gather | solution.py:70
  158.5 5.0 %convolution_convert_fusion = bf16[4,256,3,384]{3,1,2,0:T(8,128)(2,1)} fusion(bf16[768,3,384]{2,0,1:T(8,128)(2,1)S(1)} %copy-done, bf16[4,256,3072]{2,1,0:T(8,128)(2,1)} %all-gather.5.cloned.1.call-done, s32[]{:T(128)S(6)} %select_n.32), kind=kOutput, calls=%fused_computation.9 | convolution fusion | flops 1813118976 | bytes 5701636 | tf_op jit(solution)/shard_map/std,dhe->sthe/dot_general | solution.py:76
  163.6 0.0 reduce-scatter.2.cloned.1.call-start
  163.6 0.6 copy-done.9
  164.2 0.1 iota_compare_fusion
  164.3 90.3 %all-reduce.5.cloned.1.call-done = (bf16[4,256,3,384]{3,1,2,0:T(8,128)(2,1)}, bf16[4,128,3,256]{3,1,2,0:T(8,128)(2,1)}) async-done(((bf16[4,256,3,384]{3,1,2,0:T(8,128)(2,1)}, bf16[4,128,3,256]{3,1,2,0:T(8,128)(2,1)}), (bf16[4,256,3,384]{3,1,2,0:T(8,128)(2,1)}, bf16[4,128,3,256]{3,1,2,0:T(8,128)(2,1)})) %all-reduce.5.cloned.1.call-update) | async-done | bytes 3145744 | tf_op jit(solution)/shard_map/psum | solution.py:81
  254.6 1.4 fusion.31
  256.0 1.0 slice.70
  257.1 1.2 slice.71
  258.3 0.4 convert_element_type.65
  258.7 0.9 multiply_reduce_fusion.1
  259.6 0.2 copy-done.3
  259.9 0.3 fusion.33
  260.2 0.5 multiply_convert_fusion
  260.6 2.8 fusion
  263.4 5.8 %bitcast_convert_fusion = bf16[4,256,768]{2,1,0:T(8,128)(2,1)} fusion(f32[4,3,256,384]{3,2,1,0:T(8,128)} %get-tuple-element.25, f32[4,384]{1,0:T(4,128)S(1)} %pad_convert_fusion, bf16[4,256,3,128]{3,1,2,0:T(8,128)(2,1)S(1)} %slice.71, bf16[4,128,3,128]{3,1,2,0:T(8,128)(2,1)S(1)} %slice.70, f32[4,256,3]{1,2,0:T(4,128)S(1)} %bitcast.60, ...), kind=kOutput, calls=%fused_computation.5 | convolution fusion | flops 913440768 | bytes 8079360 | tf_op jit(solution)/shard_map/sqhe,hed->sqd/dot_general | solution.py:100
  269.2 32.7 %reduce-scatter.2.cloned.1.call-done = bf16[4,64,768]{2,1,0:T(8,128)(2,1)} async-done(((bf16[4,256,768]{2,1,0:T(8,128)(2,1)}), bf16[4,64,768]{2,1,0:T(8,128)(2,1)}) %reduce-scatter.2.cloned.1.call-update) | async-done | bytes 393232 | tf_op jit(solution)/shard_map/reduce_scatter | solution.py:101
  301.9 1.3 copy.18
  303.2 10.0 %all_to_all.14 = bf16[4,64,768]{2,0,1:T(4,128)(2,1)S(1)} all-to-all(bf16[4,64,768]{2,0,1:T(4,128)(2,1)S(1)} %copy.18), channel_id=1, replica_groups=mesh['batch'=32,'row'=4,'col'=4] {'col'}, dimensions={1} | all-to-all | bytes 786432 | tf_op jit(solution)/shard_map/all_to_all | solution.py:104
  313.2 1.2 copy.26
  314.4 1.5 reshape.111
  316.0 0.2 fusion.52
  316.2 0.2 multiply_reduce_fusion.2
  316.5 1.4 fusion.46
  317.9 0.1 stack_reshape.2
  318.0 0.9 stack.3
  318.9 15.3 %all-to-all-start.1 = ((f32[32,4,1024]{2,1,0:T(4,128)}), f32[32,4,1024]{2,1,0:T(4,128)S(1)}, u32[]{:S(2)}, u32[]{:S(2)}) async-start(f32[32,4,1024]{2,1,0:T(4,128)} %stack.3), calls=%async_computation.2 | async-start | bytes 1048576 | tf_op jit(solution)/shard_map/all_to_all | solution.py:54
  334.2 1.3 dynamic-slice
  336.2 0.2 dynamic-update-slice
  336.4 61.7 %all-reduce.1 = f32[128]{0:T(128)S(1)} all-reduce(f32[128]{0:T(128)S(1)} %dynamic-update-slice), channel_id=1, replica_groups=mesh['batch'=32,'row'=4,'col'=4] {'batch'}, use_global_device_ids=true, to_apply=%add.1 | all-reduce | flops 128 | bytes 1024
  398.2 0.6 gather_fusion.1
  398.8 0.2 reshape.110
  399.0 0.6 gather_fusion
  399.6 0.1 gather.11
  399.7 0.2 multiply_reduce_fusion.3
  399.9 0.7 multiply_add_fusion
  (39 shorter events, 0.2 us)
Async XLA Ops:
  6.5 152.0 %copy-start = (bf16[768,3,384]{2,0,1:T(8,128)(2,1)S(1)}, bf16[768,3,384]{2,0,1:T(8,128)(2,1)}, u32[]{:S(2)}) copy-start(bf16[768,3,384]{2,0,1:T(8,128)(2,1)} %param.16) | copy-start | bytes 5308420
  6.5 6.3 %copy-start.1 = (bf16[4,16,3072]{2,1,0:T(8,128)(2,1)S(1)}, bf16[4,16,3072]{2,1,0:T(8,128)(2,1)}, u32[]{:S(2)}) copy-start(bf16[4,16,3072]{2,1,0:T(8,128)(2,1)} %param.13) | copy-start | bytes 1179652
  6.5 73.0 %all-gather.3.cloned.1.call-start = ((), (), s32[]{:S(2)}) async-start(), calls=%async_computation.3 | async-start | bytes 3342336 | tf_op jit(solution)/shard_map/all_gather | solution.py:71
  11.7 146.9 %all-gather.5.cloned.1.call-start = ((), (), s32[]{:S(2)}) async-start(), calls=%async_computation.4 | async-start | bytes 6684672 | tf_op jit(solution)/shard_map/all_gather | solution.py:70
  14.1 240.5 %all-reduce.5.cloned.1.call-start = ((), (), s32[]{:S(2)}) async-start(), calls=%async_computation.6 | async-start | bytes 6291456 | tf_op jit(solution)/shard_map/psum | solution.py:81
  163.5 0.7 copy-start.9
  163.5 0.7 copy-start.5
  163.6 138.4 %reduce-scatter.2.cloned.1.call-start = ((), (), s32[]{:S(2)}) async-start(), calls=%async_computation.5 | async-start | bytes 1966080 | tf_op jit(solution)/shard_map/reduce_scatter | solution.py:101
  254.6 3.7 copy-start.2
  258.7 1.1 copy-start.3
  316.2 20.0 %copy-start.7 = (f32[4]{0:T(128)S(1)}, f32[4]{0:T(128)}, u32[]{:S(2)}) copy-start(f32[4]{0:T(128)} %param.23) | copy-start | bytes 52
  316.2 82.0 %copy-start.8 = (s32[4]{0:T(128)S(1)}, s32[4]{0:T(128)}, u32[]{:S(2)}) copy-start(s32[4]{0:T(128)} %param.22) | copy-start | bytes 52
  316.4 83.4 %copy-start.4 = (f32[4,16,64]{2,1,0:T(8,128)S(1)}, f32[4,16,64]{2,1,0:T(8,128)}, u32[]{:S(2)}) copy-start(f32[4,16,64]{2,1,0:T(8,128)} %param.25) | copy-start | bytes 49156
  316.5 83.4 %copy-start.6 = (f32[4]{0:T(128)S(1)}, f32[4]{0:T(128)}, u32[]{:S(2)}) copy-start(f32[4]{0:T(128)} %param.24) | copy-start | bytes 52
  318.9 80.0 %all-to-all-start.1 = ((f32[32,4,1024]{2,1,0:T(4,128)}), f32[32,4,1024]{2,1,0:T(4,128)S(1)}, u32[]{:S(2)}, u32[]{:S(2)}) async-start(f32[32,4,1024]{2,1,0:T(4,128)} %stack.3), calls=%async_computation.2 | async-start | bytes 1048576 | tf_op jit(solution)/shard_map/all_to_all | solution.py:54
Sparse Core Ops, SparseCore 0:
  11.8 67.7 all-gather.2
  82.6 75.8 all-gather.4
  163.7 90.8 all-reduce.4
  269.3 32.5 reduce-scatter.1
